TPU v7x, 256 devices: a whole 4x4x8 slice. The times are simulated.
256 devices in a mesh: batch: 64 (over x, z, core), proto: 4 (over y).
Axes of the slice: x: 4, y: 4, z: 8, core: 2. Of those that a mesh axis runs over, the one named last changes fastest.
Arguments:
- embeddings: bfloat16 [16384, 256], P('batch'), may hold values from -64 to 64
- prototypes: bfloat16 [65536, 256], P('proto'), may hold values from -1 to 1
- row_cot: float32 [16384], P('batch'), may hold values from -6 to 6
- col_cot: float32 [65536], P('proto'), may hold values from -6 to 6
Outputs:
- embed_grad: float32 [16384, 256], P('batch')
- proto_grad: float32 [65536, 256], P(('proto', 'batch'))
All inputs are finite; a program needn't handle non-finite values.
Results may differ from a plain program's by a relative error of at most 0.0033.
Values may be sent and summed in bfloat16 or wider, within the bound.
A program may use at most 128 MiB of HBM per device.

v0:
```python
import math

import jax
import jax.numpy as jnp
from jax import lax
from jax.sharding import Mesh
from jax.sharding import PartitionSpec as P

BATCH = ("batch_0", "batch_1", "batch_2")
PROTO_BATCH = ("proto", "batch_0", "batch_1", "batch_2")


score_scale = 4.0


def sent_to_all(x, axis):
    length = lax.axis_size(axis)
    return lax.all_to_all(jnp.broadcast_to(x[None], (length, *x.shape)), axis, 0, 0, tiled=True)


def all_in_one(x, axis):
    leaves = jax.tree.leaves(x)
    order = sorted(range(len(leaves)), key=lambda k: -leaves[k].size)
    width = (1, *leaves[order[0]].shape)[-1]
    lines = [
        jnp.pad(leaves[k].reshape(-1), (0, -leaves[k].size % width)).reshape(-1, width)
        for k in order
    ]
    both, at, found = (sent_to_all(jnp.concatenate(lines), axis), 0, {})
    for k, line in zip(order, lines):
        piece = both[:, at : at + len(line)].reshape(len(both), -1)
        found[k] = piece[:, : leaves[k].size].reshape(-1, *leaves[k].shape)
        at += len(line)
    numbers = iter(range(len(leaves)))
    return jax.tree.map(lambda _: found[next(numbers)], x)


def collected_alike(x, axis):
    leaves, found = (jax.tree.leaves(x), {})
    for first, a in enumerate(leaves):
        if first not in found:
            alike = [k for k, b in enumerate(leaves) if b.dtype == a.dtype]
            got = (
                all_in_one([leaves[k] for k in alike], axis)
                if len(alike) > 1
                else [sent_to_all(a, axis)]
            )
            for k, b in zip(alike, got):
                found[k] = b
    numbers = iter(range(len(leaves)))
    return jax.tree.map(lambda _: found[next(numbers)], x)


def folded_in_pairs(pieces, combine):
    while len(jax.tree.leaves(pieces)[0]) > 1:
        pieces = jax.vmap(combine)(
            *(jax.tree.map(lambda part: part[side::2], pieces) for side in (0, 1))
        )
    return jax.tree.map(lambda part: part[0], pieces)


def joined_all(x, axis, combine):
    pieces = collected_alike(x, axis)
    return folded_in_pairs(pieces, combine)


def merged_by_axis(x, axes, combine):
    for axis in axes:
        pieces = jax.tree.map(lambda part: lax.all_gather(part, axis), x)
        x = jax.tree.map(lambda part: part[0], pieces)
        for k in range(1, lax.axis_size(axis)):
            x = combine(x, jax.tree.map(lambda part: part[k], pieces))
    return x


def of_everyone(x, axis):
    everything = sent_to_all(x, axis)
    return jnp.sum(everything, axis=0)


def over_pieces(x, axis):
    parts = lax.all_gather(x, axis)
    return parts.sum(axis=0)


def pair_combine(first, second):
    top = jnp.maximum(first[0], second[0])
    return (top, first[1] * jnp.exp(first[0] - top) + second[1] * jnp.exp(second[0] - top))


def row_lse(scores, col_pot):
    shifted = scores + col_pot[None, :]
    local_peak = jnp.max(shifted, axis=1)
    local_mass = jnp.sum(jnp.exp(shifted - local_peak[:, None]), axis=1)
    peak, mass = joined_all((local_peak, local_mass), "proto", pair_combine)
    return peak + jnp.log(mass)


def col_lse(scores, row_pot):
    shifted = scores + row_pot[:, None]
    local_peak = jnp.max(shifted, axis=0)
    local_mass = jnp.sum(jnp.exp(shifted - local_peak[None, :]), axis=0)
    peak, mass = merged_by_axis((local_peak, local_mass), BATCH, pair_combine)
    return peak + jnp.log(mass)


def row_total(values):
    return of_everyone(values, "proto")


def shards(embeddings, prototypes, row_cot, col_cot):
    log_rows = math.log(embeddings.shape[0] * lax.axis_size(BATCH))
    log_cols = math.log(prototypes.shape[0] * lax.axis_size("proto"))
    scores = (
        lax.dot_general(
            embeddings, prototypes, (((1,), (1,)), ((), ())), preferred_element_type=jnp.float32
        )
        * score_scale
    )
    f_one = -log_rows - row_lse(scores, jnp.zeros((scores.shape[1],), jnp.float32))
    g_one = -log_cols - col_lse(scores, f_one)
    f_two = -log_rows - row_lse(scores, g_one)
    g_two = -log_cols - col_lse(scores, f_two)
    plan_four = jnp.exp(scores + f_two[:, None] + g_two[None, :] + log_cols)
    bar_ftwo = row_cot - row_total(jnp.sum(plan_four * col_cot[None, :], axis=1))
    plan_three = jnp.exp(scores + f_two[:, None] + g_one[None, :] + log_rows)
    bar_gone = -over_pieces(jnp.sum(bar_ftwo[:, None] * plan_three, axis=0), BATCH)
    plan_two = jnp.exp(scores + f_one[:, None] + g_one[None, :] + log_cols)
    bar_fone = -row_total(jnp.sum(plan_two * bar_gone[None, :], axis=1))
    plan_one = jnp.exp(scores + f_one[:, None] + log_rows)
    adjoint = -(
        col_cot[None, :] * plan_four
        + bar_ftwo[:, None] * plan_three
        + bar_gone[None, :] * plan_two
        + bar_fone[:, None] * plan_one
    )
    adjoint = adjoint.astype(jnp.bfloat16)
    row_part = jnp.dot(adjoint, prototypes, preferred_element_type=jnp.float32) * score_scale
    embed_grad = of_everyone(row_part, "proto")
    product = lax.dot_general(
        adjoint, embeddings, (((0,), (0,)), ((), ())), preferred_element_type=jnp.float32
    )
    proto_grad = lax.psum_scatter(product * score_scale, BATCH, scatter_dimension=0, tiled=True)
    return (embed_grad, proto_grad)


def solution(mesh):
    split = Mesh(
        mesh.devices.reshape(4, 8, 2, mesh.shape["proto"]),
        ("batch_0", "batch_1", "batch_2", "proto"),
    )
    return jax.shard_map(
        shards,
        mesh=split,
        in_specs=(P(BATCH, None), P("proto", None), P(BATCH), P("proto")),
        out_specs=(P(BATCH, None), P(PROTO_BATCH, None)),
        check_vma=False,
    )
```

profile of v0, /device:TPU:1, one launch (start us, length us, event | category | flops | bytes accessed | tf_op | source)
XLA Modules:
  0.0 605.2 jit_solution(10974719053967261115)
XLA Ops:
  7.2 0.8 copy-done
  8.1 11.5 %fusion.65 = (f32[256]{0:T(256)S(1)}, f32[256,16384]{1,0:T(8,128)}) fusion(bf16[256,256]{1,0:T(8,128)(2,1)S(1)} %copy-done, bf16[16384,256]{1,0:T(8,128)(2,1)} %param.5), kind=kOutput, calls=%fused_computation.145 | convolution fusion | flops 2155872000 | bytes 25297920 | tf_op jit(solution)/shard_map/dot_general | solution.py:115
  19.6 8.1 %exponential_reduce_fusion.3 = f32[256]{0:T(256)S(1)} fusion(f32[256,16384]{1,0:T(8,128)} %get-tuple-element.31, f32[256]{0:T(256)S(1)} %get-tuple-element.30), kind=kLoop, calls=%fused_computation.10 | loop fusion | flops 8388352 | bytes 16779264 | tf_op jit(solution)/shard_map/reduce_sum | solution.py:94
  27.7 9.0 %all_to_all.27 = f32[4,2,256]{2,1,0:T(2,128)S(1)} all-to-all(f32[4,2,256]{2,1,0:T(2,128)S(1)} %broadcast_in_dim.10), channel_id=1, replica_groups=mesh['batch_0'=4,'batch_1'=8,'batch_2'=2,'proto'=4] {'proto'}, dimensions={0} | all-to-all | bytes 16384 | tf_op jit(solution)/shard_map/all_to_all | solution.py:18
  36.9 7.6 %add_reduce_fusion.2 = f32[16384]{0:T(1024)S(1)} fusion(f32[256,16384]{1,0:T(8,128)} %get-tuple-element.31, f32[256]{0:T(256)S(1)} %bitcast.404), kind=kLoop, calls=%fused_computation.13 | loop fusion | flops 8372224 | bytes 16843776 | tf_op jit(solution)/shard_map/reduce_max | solution.py:101
  44.5 8.7 %exponential_reduce_fusion.2 = f32[16384]{0:T(1024)S(1)} fusion(f32[256,16384]{1,0:T(8,128)} %get-tuple-element.31, f32[16384]{0:T(1024)S(1)} %add_reduce_fusion.2, f32[256]{0:T(256)S(1)} %bitcast.405), kind=kLoop, calls=%fused_computation.9 | loop fusion | flops 12566528 | bytes 16909312 | tf_op jit(solution)/shard_map/reduce_sum | solution.py:102
  53.2 9.7 %all-gather = f32[65536]{0:T(1024)S(1)} all-gather(f32[16384]{0:T(1024)S(1)} %add_reduce_fusion.2), channel_id=2, replica_groups=mesh['batch_0'=4,'batch_1'=8,'batch_2'=2,'proto'=4] {'batch_0'}, dimensions={0}, use_global_device_ids=true | all-gather | bytes 327680 | tf_op jit(solution)/shard_map/all_gather | solution.py:69
  62.9 9.8 %all-gather.1 = f32[65536]{0:T(1024)S(1)} all-gather(f32[16384]{0:T(1024)S(1)} %exponential_reduce_fusion.2), channel_id=3, replica_groups=mesh['batch_0'=4,'batch_1'=8,'batch_2'=2,'proto'=4] {'batch_0'}, dimensions={0}, use_global_device_ids=true | all-gather | bytes 327680 | tf_op jit(solution)/shard_map/all_gather | solution.py:69
  72.7 0.5 maximum_bitcast_fusion.3
  73.2 23.4 %all-gather.5 = f32[8,1,16384]{2,1,0:T(1,128)S(1)} all-gather(f32[1,1,16384]{2,1,0:T(1,128)S(1)} %get-tuple-element.16), channel_id=1, replica_groups=mesh['batch_0'=4,'batch_1'=8,'batch_2'=2,'proto'=4] {'batch_1'}, dimensions={0}, use_global_device_ids=true | all-gather | bytes 589824 | tf_op jit(solution)/shard_map/all_gather | solution.py:69
  96.6 0.2 maximum_bitcast_fusion.2
  96.8 15.0 %all-gather.6 = f32[2,1,16384]{2,1,0:T(1,128)S(1)} all-gather(f32[1,1,16384]{2,1,0:T(1,128)S(1)} %maximum_bitcast_fusion.2), channel_id=1, replica_groups=mesh['batch_0'=4,'batch_1'=8,'batch_2'=2,'proto'=4] {'batch_2'}, dimensions={0}, use_global_device_ids=true | all-gather | bytes 196608 | tf_op jit(solution)/shard_map/all_gather | solution.py:69
  111.8 20.0 %all-gather.7 = f32[8,1,16384]{2,1,0:T(1,128)S(1)} all-gather(f32[1,1,16384]{2,1,0:T(1,128)S(1)} %get-tuple-element.17), channel_id=1, replica_groups=mesh['batch_0'=4,'batch_1'=8,'batch_2'=2,'proto'=4] {'batch_1'}, dimensions={0}, use_global_device_ids=true | all-gather | bytes 589824 | tf_op jit(solution)/shard_map/all_gather | solution.py:69
  131.7 1.2 fusion.53
  132.9 7.8 %all-gather.8 = f32[2,1,16384]{2,1,0:T(1,128)S(1)} all-gather(f32[1,1,16384]{2,1,0:T(1,128)S(1)} %fusion.53), channel_id=1, replica_groups=mesh['batch_0'=4,'batch_1'=8,'batch_2'=2,'proto'=4] {'batch_2'}, dimensions={0}, use_global_device_ids=true | all-gather | bytes 196608 | tf_op jit(solution)/shard_map/all_gather | solution.py:69
  140.7 0.3 add_subtract_fusion.1
  141.0 7.2 %add_reduce_fusion = f32[256]{0:T(256)S(1)} fusion(f32[256,16384]{1,0:T(8,128)} %get-tuple-element.31, f32[16384]{0:T(1024)S(1)} %bitcast.376), kind=kLoop, calls=%fused_computation.11 | loop fusion | flops 8388352 | bytes 16843776 | tf_op jit(solution)/shard_map/reduce_max | solution.py:93
  148.2 8.7 %exponential_reduce_fusion.1 = f32[256]{0:T(256)S(1)} fusion(f32[256,16384]{1,0:T(8,128)} %get-tuple-element.31, f32[256]{0:T(256)S(1)} %add_reduce_fusion, f32[16384]{0:T(1024)S(1)} %bitcast.377), kind=kLoop, calls=%fused_computation.8 | loop fusion | flops 12582656 | bytes 16844800 | tf_op jit(solution)/shard_map/reduce_sum | solution.py:94
  156.9 6.5 %all_to_all.28 = f32[4,2,256]{2,1,0:T(2,128)S(1)} all-to-all(f32[4,2,256]{2,1,0:T(2,128)S(1)} %broadcast_in_dim.11), channel_id=1, replica_groups=mesh['batch_0'=4,'batch_1'=8,'batch_2'=2,'proto'=4] {'proto'}, dimensions={0} | all-to-all | bytes 16384 | tf_op jit(solution)/shard_map/all_to_all | solution.py:18
  163.6 7.7 %add_reduce_fusion.1 = f32[16384]{0:T(1024)S(1)} fusion(f32[256,16384]{1,0:T(8,128)} %get-tuple-element.31, f32[256]{0:T(256)S(1)} %bitcast.399), kind=kLoop, calls=%fused_computation.12 | loop fusion | flops 8372224 | bytes 16843776 | tf_op jit(solution)/shard_map/reduce_max | solution.py:101
  171.2 8.7 %exponential_reduce_fusion = f32[16384]{0:T(1024)S(1)} fusion(f32[256,16384]{1,0:T(8,128)} %get-tuple-element.31, f32[16384]{0:T(1024)S(1)} %add_reduce_fusion.1, f32[256]{0:T(256)S(1)} %bitcast.400), kind=kLoop, calls=%fused_computation.7 | loop fusion | flops 12566528 | bytes 16909312 | tf_op jit(solution)/shard_map/reduce_sum | solution.py:102
  179.9 9.4 %all-gather.2 = f32[65536]{0:T(1024)S(1)} all-gather(f32[16384]{0:T(1024)S(1)} %add_reduce_fusion.1), channel_id=4, replica_groups=mesh['batch_0'=4,'batch_1'=8,'batch_2'=2,'proto'=4] {'batch_0'}, dimensions={0}, use_global_device_ids=true | all-gather | bytes 327680 | tf_op jit(solution)/shard_map/all_gather | solution.py:69
  189.3 10.0 %all-gather.3 = f32[65536]{0:T(1024)S(1)} all-gather(f32[16384]{0:T(1024)S(1)} %exponential_reduce_fusion), channel_id=5, replica_groups=mesh['batch_0'=4,'batch_1'=8,'batch_2'=2,'proto'=4] {'batch_0'}, dimensions={0}, use_global_device_ids=true | all-gather | bytes 327680 | tf_op jit(solution)/shard_map/all_gather | solution.py:69
  199.4 0.5 maximum_bitcast_fusion.1
  199.9 19.1 %all-gather.9 = f32[8,1,16384]{2,1,0:T(1,128)S(1)} all-gather(f32[1,1,16384]{2,1,0:T(1,128)S(1)} %get-tuple-element.6), channel_id=1, replica_groups=mesh['batch_0'=4,'batch_1'=8,'batch_2'=2,'proto'=4] {'batch_1'}, dimensions={0}, use_global_device_ids=true | all-gather | bytes 589824 | tf_op jit(solution)/shard_map/all_gather | solution.py:69
  219.0 0.2 maximum_bitcast_fusion
  219.2 14.9 %all-gather.10 = f32[2,1,16384]{2,1,0:T(1,128)S(1)} all-gather(f32[1,1,16384]{2,1,0:T(1,128)S(1)} %maximum_bitcast_fusion), channel_id=1, replica_groups=mesh['batch_0'=4,'batch_1'=8,'batch_2'=2,'proto'=4] {'batch_2'}, dimensions={0}, use_global_device_ids=true | all-gather | bytes 196608 | tf_op jit(solution)/shard_map/all_gather | solution.py:69
  234.2 19.4 %all-gather.11 = f32[8,1,16384]{2,1,0:T(1,128)S(1)} all-gather(f32[1,1,16384]{2,1,0:T(1,128)S(1)} %get-tuple-element.7), channel_id=1, replica_groups=mesh['batch_0'=4,'batch_1'=8,'batch_2'=2,'proto'=4] {'batch_1'}, dimensions={0}, use_global_device_ids=true | all-gather | bytes 589824 | tf_op jit(solution)/shard_map/all_gather | solution.py:69
  253.6 1.2 fusion.54
  254.7 7.9 %all-gather.12 = f32[2,1,16384]{2,1,0:T(1,128)S(1)} all-gather(f32[1,1,16384]{2,1,0:T(1,128)S(1)} %fusion.54), channel_id=1, replica_groups=mesh['batch_0'=4,'batch_1'=8,'batch_2'=2,'proto'=4] {'batch_2'}, dimensions={0}, use_global_device_ids=true | all-gather | bytes 196608 | tf_op jit(solution)/shard_map/all_gather | solution.py:69
  262.7 0.3 add_subtract_fusion
  262.9 8.1 %fusion.1 = f32[256]{0:T(256)S(1)} fusion(f32[256,16384]{1,0:T(8,128)} %get-tuple-element.31, f32[16384]{0:T(1024)S(1)} %bitcast.381, f32[256]{0:T(256)S(1)} %bitcast.401, f32[16384]{0:T(1024)S(1)} %copy-done.2), kind=kLoop, calls=%fused_computation.14 | loop fusion | flops 20971264 | bytes 16910336 | tf_op jit(solution)/shard_map/reduce_sum | solution.py:125
  271.0 6.5 %all_to_all.29 = f32[4,1,256]{2,1,0:T(1,128)S(1)} all-to-all(f32[4,1,256]{2,1,0:T(1,128)S(1)} %broadcast_in_dim.12), channel_id=1, replica_groups=mesh['batch_0'=4,'batch_1'=8,'batch_2'=2,'proto'=4] {'proto'}, dimensions={0} | all-to-all | bytes 8192 | tf_op jit(solution)/shard_map/all_to_all | solution.py:18
  277.6 8.8 %fusion.2 = f32[16384]{0:T(1024)} fusion(f32[256,16384]{1,0:T(8,128)} %get-tuple-element.31, f32[256]{0:T(256)S(1)} %sub.329, f32[256]{0:T(256)S(1)} %bitcast.402, f32[16384]{0:T(1024)S(1)} %bitcast.378), kind=kLoop, calls=%fused_computation.15 | loop fusion | flops 20955136 | bytes 16910336 | tf_op jit(solution)/shard_map/reduce_sum | solution.py:127
  286.4 0.0 reduce-scatter.2.cloned.1.call-start
  286.4 76.7 %all-gather.15.cloned.1.call-done = f32[1048576]{0:T(1024)} async-done(((f32[16384]{0:T(1024)}), f32[1048576]{0:T(1024)}) %all-gather.15.cloned.1.call-update) | async-done | bytes 4194320 | tf_op jit(solution)/shard_map/all_gather | solution.py:82
  363.1 5.0 reshape.97
  368.1 2.5 reduce_sum.106
  370.6 8.1 %fusion = f32[256]{0:T(256)S(1)} fusion(f32[256,16384]{1,0:T(8,128)} %get-tuple-element.31, f32[16384]{0:T(1024)S(1)} %neg.17, f32[16384]{0:T(1024)S(1)} %bitcast.379, f32[256]{0:T(256)S(1)} %bitcast.406), kind=kLoop, calls=%fused_computation.4 | loop fusion | flops 20971264 | bytes 16910336 | tf_op jit(solution)/shard_map/reduce_sum | solution.py:129
  378.7 8.2 %all_to_all.30 = f32[4,1,256]{2,1,0:T(1,128)S(1)} all-to-all(f32[4,1,256]{2,1,0:T(1,128)S(1)} %broadcast_in_dim.13), channel_id=1, replica_groups=mesh['batch_0'=4,'batch_1'=8,'batch_2'=2,'proto'=4] {'proto'}, dimensions={0} | all-to-all | bytes 8192 | tf_op jit(solution)/shard_map/all_to_all | solution.py:18
  386.9 17.5 %negate_convert_fusion = bf16[256,16384]{1,0:T(8,128)(2,1)S(1)} fusion(f32[256,16384]{1,0:T(8,128)} %get-tuple-element.31, f32[256]{0:T(256)S(1)} %neg.18, f32[16384]{0:T(1024)S(1)} %neg.17, f32[256]{0:T(256)S(1)} %sub.329, f32[16384]{0:T(1024)S(1)} %bitcast.382, f32[256]{0:T(256)S(1)} %bitcast.403, f32[16384]{0:T(1024)S(1)} %bitcast.380, ...), kind=kLoop, calls=%fused_computation.2 | loop fusion | flops 75497472 | bytes 25432064 | tf_op jit(solution)/shard_map/convert_element_type | solution.py:137
  404.4 3.2 copy-done.1
  407.6 8.2 %convolution_multiply_fusion.1 = f32[16384,256]{1,0:T(8,128)} fusion(bf16[256,16384]{1,0:T(8,128)(2,1)S(1)} %negate_convert_fusion, bf16[256,256]{1,0:T(8,128)(2,1)S(1)} %copy-done), kind=kOutput, calls=%fused_computation.1 | convolution fusion | flops 2151677952 | bytes 25296896 | tf_op jit(solution)/shard_map/dot_general | solution.py:140
  415.8 8.1 %convolution_multiply_fusion.2 = f32[256,256]{1,0:T(8,128)S(1)} fusion(bf16[256,16384]{1,0:T(8,128)(2,1)} %copy-done.1, bf16[16384,256]{1,0:T(8,128)(2,1)} %param.5), kind=kOutput, calls=%fused_computation.16 | convolution fusion | flops 2147549184 | bytes 17039360 | tf_op jit(solution)/shard_map/dot_general | solution.py:138
  423.9 0.1 broadcast_in_dim.14
  424.0 15.9 %all_to_all.31 = f32[4,256,256]{2,1,0:T(8,128)S(1)} all-to-all(f32[4,256,256]{2,1,0:T(8,128)S(1)} %broadcast_in_dim.14), channel_id=1, replica_groups=mesh['batch_0'=4,'batch_1'=8,'batch_2'=2,'proto'=4] {'proto'}, dimensions={0} | all-to-all | bytes 2097152 | tf_op jit(solution)/shard_map/all_to_all | solution.py:18
  439.9 0.8 reduce_sum.109
  440.7 157.4 %reduce-scatter.2.cloned.1.call-done = f32[256,256]{1,0:T(8,128)} async-done(((f32[16384,256]{1,0:T(8,128)}), f32[256,256]{1,0:T(8,128)}) %reduce-scatter.2.cloned.1.call-update) | async-done | bytes 262160 | tf_op jit(solution)/shard_map/reduce_scatter | solution.py:143
  (41 shorter events, 0.6 us)
Async XLA Ops:
  7.2 0.9 copy-start
  7.2 355.9 %all-gather.15.cloned.1.call-start = ((), (), s32[]{:S(2)}) async-start(), calls=%async_computation.7 | async-start | bytes 4259840 | tf_op jit(solution)/shard_map/all_gather | solution.py:82
  163.5 99.4 %copy-start.2 = (f32[16384]{0:T(1024)S(1)}, f32[16384]{0:T(1024)}, u32[]{:S(2)}) copy-start(f32[16384]{0:T(1024)} %param.7) | copy-start | bytes 196612
  171.2 106.3 %copy-start.3 = (f32[256]{0:T(256)S(1)}, f32[256]{0:T(256)}, u32[]{:S(2)}) copy-start(f32[256]{0:T(256)} %param.6) | copy-start | bytes 3076
  286.4 311.7 %reduce-scatter.2.cloned.1.call-start = ((), (), s32[]{:S(2)}) async-start(), calls=%async_computation.6 | async-start | bytes 17039360 | tf_op jit(solution)/shard_map/reduce_scatter | solution.py:143
  404.4 3.2 copy-start.1
Sparse Core Ops, SparseCore 0:
  286.5 76.5 all-gather.14
  416.0 182.1 reduce-scatter.1
where the time goes:
time: 617 us; the launch traced here: 605 us
  waiting for transfers between devices  234 us (38%)
  blocking collectives  212 us (34%)
  other arithmetic  107 us (17%)
  matrix products  27.7 us (4%)
  between operations  14.5 us (2%)
  local copies, waits for them, and re-layouts  9.45 us (2%)
    all_gather x12, blocking collectives, merged_by_axis(): pieces = jax.tree.map(lambda part: lax.all_gather(part, axis), x)  166 us
    reduce_scatter x1, waiting for transfers between devices, shards(): lax.psum_scatter(product * score_scale, BATCH, scatter_dimension=0, tiled...  157 us
    all_gather x1, waiting for transfers between devices, over_pieces(): parts = lax.all_gather(x, axis)  76.7 us
    all_to_all x5, blocking collectives, sent_to_all(): lax.all_to_all(jnp.broadcast_to(x[None], (length, *x.shape)), axis, 0, 0,...  46 us
    convert_element_type x1, other arithmetic, shards(): adjoint = adjoint.astype(jnp.bfloat16)  17.5 us
    reduce_sum x2, other arithmetic, col_lse(): local_mass = jnp.sum(jnp.exp(shifted - local_peak[None, :]), axis=0)  17.3 us
    reduce_sum x2, other arithmetic, row_lse(): local_mass = jnp.sum(jnp.exp(shifted - local_peak[:, None]), axis=1)  16.8 us
    reduce_max x2, other arithmetic, col_lse(): local_peak = jnp.max(shifted, axis=0)  15.3 us
  transfers between devices with their start and end apart: 2, of which 2 were waited for; matrix products, arithmetic and copies ran while one was open for 1% of the time, Pallas kernels for 0%

commit v1 on v0

v1 whole, which is shorter than its diff:
```python
import math

import jax
import jax.numpy as jnp
from jax import lax
from jax.experimental import pallas as pl
from jax.experimental.pallas import tpu as pltpu
from jax.sharding import Mesh
from jax.sharding import PartitionSpec as P

MESH = pl.DeviceIdType.MESH
LOG2E = math.log2(math.e)
SCALE = 4.0
SCALE2 = SCALE * LOG2E
F32 = jnp.float32
BF16 = jnp.bfloat16
NX, NZ, NC, NY = 4, 8, 2, 4
ROWS, COLS, D = 256, 16384, 256
TILES = COLS // 128
LOG2_B = math.log2(ROWS * NX * NZ * NC)
N_B = float(ROWS * NX * NZ * NC)
N_K = float(COLS * NY)


def dot_nt(a, b):
    return lax.dot_general(a, b, (((1,), (1,)), ((), ())), preferred_element_type=F32)


def lse2(parts):
    top = parts[0]
    for p in parts[1:]:
        top = jnp.maximum(top, p)
    mass = jnp.exp2(parts[0] - top)
    for p in parts[1:]:
        mass = mass + jnp.exp2(p - top)
    return top + jnp.log(mass) * LOG2E


def total(parts):
    out = parts[0]
    for p in parts[1:]:
        out = out + p
    return out


def row_form(acc):
    return jnp.sum(acc.T, axis=0, keepdims=True)


def spread(row):
    return jnp.broadcast_to(row, (128, row.shape[1])).T


def kernel(emb_hbm, protos_hbm, rcot_ref, ccot_ref, eg_ref, pg_ref,
           S, PV, EA, MX, FB, UB, XB, CM, CS, W, A, H, LG, V, ADJ, RP, PG, PR, LB, AB, CB, DB, ADJ2,
           rbuf, cloc, c1, c2, c3, G, Y, EB, EO,
           psem, esem, rs, rr, s1, r1, s2, r2, s3, r3, es_z, es_x, er, gs, gr, ys, yr, eb_s, eb_r, eo_s, eo_r, pr_s, pr_r):
    x, z, c, y = lax.axis_index("x"), lax.axis_index("z"), lax.axis_index("c"), lax.axis_index("p")
    k = x * NC + c
    sent = []

    def send(src, dst, ssem, rsem, where):
        copy = pltpu.make_async_remote_copy(src_ref=src, dst_ref=dst, send_sem=ssem, recv_sem=rsem,
                                            device_id=where, device_id_type=MESH)
        copy.start()
        sent.append(copy)

    def landed(ref, ssem, rsem, where):
        pltpu.make_async_remote_copy(src_ref=ref, dst_ref=ref, send_sem=ssem, recv_sem=rsem,
                                     device_id=where, device_id_type=MESH).wait_recv()

    def at_y(d):
        return (y + d) % NY

    def at_z(d):
        return (z + d) % NZ

    def at_x(d):
        return (x + d) % NX

    def at_k(d):
        return (k + d) % (NX * NC)

    def xc(kk):
        return {"x": kk // NC, "c": kk % NC}

    barrier = pltpu.get_barrier_semaphore()
    for d in range(1, NY):
        pl.semaphore_signal(barrier, inc=1, device_id={"p": at_y(d)}, device_id_type=MESH)
    for d in range(1, NX * NC):
        pl.semaphore_signal(barrier, inc=1, device_id=xc(at_k(d)), device_id_type=MESH)
    for d in range(1, NZ):
        pl.semaphore_signal(barrier, inc=1, device_id={"z": at_z(d)}, device_id_type=MESH)

    own = pltpu.make_async_copy(emb_hbm, EA.at[x, z], esem)
    own.start()
    step = COLS // 8
    loads = [pltpu.make_async_copy(protos_hbm.at[pl.ds(q * step, step)], PV.at[pl.ds(q * step, step)], psem.at[q])
             for q in range(8)]
    for q in loads:
        q.start()
    MX[...] = jnp.full((ROWS, 128), -jnp.inf, F32)
    own.wait()

    def score_chunk(q, _):
        at = pl.multiple_of(q * 512, 512)
        s = dot_nt(EA[x, z], PV[pl.ds(at, 512), :]) * SCALE2
        m = MX[...]
        for j in range(4):
            t = s[:, j * 128:(j + 1) * 128]
            S[4 * q + j] = t
            m = jnp.maximum(m, t)
        MX[...] = m
        return 0

    def x_stage(r):
        zb = at_z(r)
        if r:
            landed(EA.at[x, zb], es_z.at[r], er.at[x, zb], {"z": zb})
        for d in range(1, NX):
            send(EA.at[x, zb], EA.at[x, zb], es_x.at[r, d], er.at[x, zb], {"x": at_x(d)})

    def z_stage(d):
        send(EA.at[x, z], EA.at[x, z], es_z.at[NZ - d], er.at[x, z], {"z": at_z(d)})

    for q in range(8):
        loads[q].wait()
        lax.fori_loop(q * 4, q * 4 + 4, score_chunk, 0)
        if q == 3:
            pl.semaphore_wait(barrier, NY - 1 + NX * NC - 1 + NZ - 1)
            for d in (1, 7, 2, 6):
                z_stage(d)
            x_stage(0)

    def mass_tile(t, acc):
        for j in range(2):
            acc = acc + jnp.exp2(S[2 * t + j] - MX[...])
        return acc

    mass = lax.fori_loop(0, TILES // 2, mass_tile, jnp.zeros((ROWS, 128), F32))
    mt = MX[...].T
    top = jnp.max(mt, axis=0, keepdims=True)
    loc = top + jnp.log(jnp.sum(mass.T * jnp.exp2(mt - top), axis=0, keepdims=True)) * LOG2E

    def row_all(i, row, combine):
        rbuf[i, y] = row
        for d in range(1, NY):
            send(rbuf.at[i, y], rbuf.at[i, y], rs.at[i, d], rr.at[i, y], {"p": at_y(d)})
        for d in range(1, NY):
            f = at_y(d)
            landed(rbuf.at[i, f], rs.at[i, d], rr.at[i, f], {"p": f})
        return combine([rbuf[i, j] for j in range(NY)])

    def col_all(i, col, combine, between):
        cloc[i] = col.reshape(8, TILES // 8, 128)
        for d in range(1, 8):
            f = at_k(d)
            send(cloc.at[i, f], c1.at[i, k], s1.at[i, d], r1.at[i, k], xc(f))
        c1[i, k] = cloc[i, k]
        for d in range(1, 8):
            f = at_k(d)
            landed(c1.at[i, f], s1.at[i, d], r1.at[i, f], xc(f))
        c2[i, z] = combine([c1[i, j] for j in range(8)])
        for d in range(1, NZ):
            send(c2.at[i, z], c2.at[i, z], s2.at[i, d], r2.at[i, z], {"z": at_z(d)})
        between()
        for d in range(1, NZ):
            f = at_z(d)
            landed(c2.at[i, f], s2.at[i, d], r2.at[i, f], {"z": f})
        c3[i, k] = combine([c2[i, j] for j in range(NZ)])
        for d in range(1, 8):
            send(c3.at[i, k], c3.at[i, k], s3.at[i, d], r3.at[i, k], xc(at_k(d)))
        for d in range(1, 8):
            f = at_k(d)
            landed(c3.at[i, f], s3.at[i, d], r3.at[i, f], xc(f))
        return c3[i].reshape(TILES, 128)

    def row_pass():
        def tile(t, acc):
            for j in range(4):
                acc = acc + S[4 * t + j] * W[pl.ds(4 * t + j, 1), :]
            return acc
        return row_form(lax.fori_loop(0, TILES // 4, tile, jnp.zeros((ROWS, 128), F32)))

    def col_pass(weights):
        def tile(t, _):
            for j in range(2):
                CS[pl.ds(2 * t + j, 1), :] = jnp.sum(S[2 * t + j] * weights[...], axis=0, keepdims=True)
            return 0
        lax.fori_loop(0, TILES // 2, tile, 0)
        return CS[...]

    f_one = -LOG2_B - row_all(0, loc, lse2)
    FB[...] = spread(f_one)

    def plan_tile(t, _):
        v = S[t] + FB[...]
        m = jnp.max(v, axis=0, keepdims=True)
        e = jnp.exp2(v - m)
        S[t] = e
        CM[pl.ds(t, 1), :] = m
        CS[pl.ds(t, 1), :] = jnp.sum(e, axis=0, keepdims=True)
        return 0

    lax.fori_loop(0, TILES, plan_tile, 0)
    big = col_all(0, CM[...] + jnp.log(CS[...]) * LOG2E, lse2, lambda: x_stage(1))
    LG[...] = big
    H[...] = jnp.exp2(CM[...] - big)
    for d in (3, 5):
        z_stage(d)
    x_stage(7)
    W[...] = H[...]
    u = (N_K / N_B) / row_all(1, row_pass(), total)
    UB[...] = spread(u)
    v = 1.0 / col_all(1, H[...] * col_pass(UB), total, lambda: x_stage(2))
    V[...] = -(v * ccot_ref[...])
    z_stage(4)
    x_stage(6)
    A[...] = H[...] * V[...]
    W[...] = A[...]
    bar_two = rcot_ref[...] + u * row_all(2, row_pass(), total)
    xr = bar_two * u
    XB[...] = spread(xr)
    xn = xr * -(N_B / N_K)
    for j, vec in enumerate((f_one, u, xn)):
        G[x, z, 2 * j:2 * j + 1] = vec[:, :128]
        G[x, z, 2 * j + 1:2 * j + 2] = vec[:, 128:]
    G[x, z, 6:8] = jnp.zeros((2, 128), F32)
    for d in range(1, NZ):
        send(G.at[x, z], G.at[x, z], gs.at[0, d], gr.at[x, z], {"z": at_z(d)})
    neg_bar_one = (N_B / N_K) * col_all(2, H[...] * col_pass(XB), total, lambda: x_stage(3))
    for d in range(1, NZ):
        f = at_z(d)
        landed(G.at[x, f], gs.at[0, d], gr.at[x, f], {"z": f})
    for d in range(1, NX):
        send(G.at[x], G.at[x], gs.at[1, d], yr.at[0, x], {"x": at_x(d)})
    x_stage(5)
    x_stage(4)
    CS[...] = neg_bar_one
    W[...] = H[...] * neg_bar_one
    yn = -row_all(3, row_pass(), total)
    Y[x, z, 0:1] = yn[:, :128]
    Y[x, z, 1:2] = yn[:, 128:]
    for d in range(1, NZ):
        send(Y.at[x, z], Y.at[x, z], ys.at[0, d], gr.at[NX + x, z], {"z": at_z(d)})
    XB[...] = XB[...] * -(N_B / N_K)
    FB[...] = spread(yn)
    CM[...] = jnp.exp2(CM[...]) * N_B
    RP[...] = jnp.zeros((ROWS, D), F32)

    def grad_chunk(q, _):
        at = pl.multiple_of(q * 512, 512)
        for j in range(4):
            t = 4 * q + j
            g = UB[...] * A[pl.ds(t, 1), :] + XB[...] * H[pl.ds(t, 1), :]
            g = g + FB[...] * CM[pl.ds(t, 1), :] + W[pl.ds(t, 1), :]
            ADJ[:, j * 128:(j + 1) * 128] = (S[t] * g).astype(BF16)
        RP[...] += jnp.dot(ADJ[...], PV[pl.ds(at, 512), :], preferred_element_type=F32)
        return 0

    half = COLS // 1024
    lax.fori_loop(0, half, grad_chunk, 0)
    for d in range(1, NZ):
        f = at_z(d)
        landed(Y.at[x, f], ys.at[0, d], gr.at[NX + x, f], {"z": f})
    for d in range(1, NX):
        send(Y.at[x], Y.at[x], ys.at[1, d], yr.at[1, x], {"x": at_x(d)})
    lax.fori_loop(half, 2 * half, grad_chunk, 0)
    piece = ROWS // NY

    def quarter(j):
        return RP.at[pl.ds(pl.multiple_of(j * piece, piece), piece)]

    for d in range(1, NY):
        f = at_y(d)
        send(quarter(f), EB.at[y], eb_s.at[d], eb_r.at[y], {"p": f})
    EB[y] = quarter(y)[...]

    chip = x * NZ + z
    pown = PV.at[pl.ds(pl.multiple_of(chip * 512, 512), 512)]
    for j in range(4):
        at = pl.ds(j * 128, 128)
        line = pl.ds(chip * 4 + j, 1)
        LB[at, :] = spread(LG[line, :])
        AB[at, :] = spread(V[line, :])
        CB[at, :] = spread(CS[line, :])
        DB[at, :] = spread(jnp.exp2(LG[line, :]) * N_B)
    PG[...] = jnp.zeros((2 * ROWS, D), F32)
    for d in range(1, NX):
        f = at_x(d)
        landed(G.at[f], gs.at[1, d], yr.at[0, f], {"x": f})
        landed(Y.at[f], ys.at[1, d], yr.at[1, f], {"x": f})
        for r in range(NZ):
            zb = at_z(r)
            landed(EA.at[f, zb], es_x.at[r, d], er.at[f, zb], {"x": f})

    def back_block(o, _):
        xb, zb = o // NZ, o % NZ
        s = dot_nt(pown[...], EA[xb, zb]) * SCALE2
        for j in range(4):
            at = slice(j * 128, (j + 1) * 128)
            for n in range(2):
                e = jnp.exp2(s[at, n * 128:(n + 1) * 128] + G[xb, zb, n:n + 1] - LB[at, :])
                g = AB[at, :] * G[xb, zb, 2 + n:3 + n] + G[xb, zb, 4 + n:5 + n]
                g = g + CB[at, :] + DB[at, :] * Y[xb, zb, n:n + 1]
                ADJ2[at, n * 128:(n + 1) * 128] = (e * g).astype(BF16)
        PG[...] += jnp.dot(ADJ2[...], EA[xb, zb], preferred_element_type=F32)
        return 0

    mid = NX * NZ // 2
    lax.fori_loop(0, mid, back_block, 0)
    for d in range(1, NY):
        f = at_y(d)
        landed(EB.at[f], eb_s.at[d], eb_r.at[f], {"p": f})
    EO[y] = total([EB[j] for j in range(NY)]) * SCALE
    for d in range(1, NY):
        send(EO.at[y], EO.at[y], eo_s.at[d], eo_r.at[y], {"p": at_y(d)})
    lax.fori_loop(mid, 2 * mid, back_block, 0)
    there = PG.at[pl.ds(pl.multiple_of((1 - c) * ROWS, ROWS), ROWS)]
    send(there, PR, pr_s, pr_r, {"c": 1 - c})
    for d in range(1, NY):
        f = at_y(d)
        landed(EO.at[f], eo_s.at[d], eo_r.at[f], {"p": f})
    eg_ref[...] = EO[...].reshape(ROWS, D)
    landed(PR, pr_s, pr_r, {"c": 1 - c})
    pg_ref[...] = (PG[pl.ds(pl.multiple_of(c * ROWS, ROWS), ROWS), :] + PR[...]) * SCALE
    for copy in sent:
        copy.wait_send()


def step(embeddings, prototypes, row_cot, col_cot):
    vm = pltpu.VMEM
    dma = pltpu.SemaphoreType.DMA
    wide = vm((ROWS, 128), F32)
    line = vm((TILES, 128), F32)
    scratch = [
        vm((TILES, ROWS, 128), F32), vm((COLS, D), BF16), vm((NX, NZ, ROWS, D), BF16),
        wide, wide, wide, wide,
        line, line, line, line, line, line, line,
        vm((ROWS, 512), BF16), vm((ROWS, D), F32), vm((2 * ROWS, D), F32), vm((ROWS, D), F32),
        vm((512, 128), F32), vm((512, 128), F32), vm((512, 128), F32), vm((512, 128), F32), vm((512, ROWS), BF16),
        vm((4, NY, 1, ROWS), F32), vm((3, 8, TILES // 8, 128), F32), vm((3, 8, TILES // 8, 128), F32),
        vm((3, NZ, TILES // 8, 128), F32), vm((3, 8, TILES // 8, 128), F32),
        vm((NX, NZ, 8, 128), F32), vm((NX, NZ, 2, 128), F32),
        vm((NY, ROWS // NY, D), F32), vm((NY, ROWS // NY, D), F32),
        dma((8,)), dma(()), dma((4, NY)), dma((4, NY)),
        dma((3, 8)), dma((3, 8)), dma((3, 8)), dma((3, 8)), dma((3, 8)), dma((3, 8)),
        dma((NZ,)), dma((NZ, NX)), dma((NX, NZ)), dma((2, NZ)), dma((2 * NX, NZ)),
        dma((2, NZ)), dma((2, NX)),
        dma((NY,)), dma((NY,)), dma((NY,)), dma((NY,)), dma(()), dma(()),
    ]
    anywhere = pl.BlockSpec(memory_space=pl.ANY)
    inside = pl.BlockSpec(memory_space=pltpu.VMEM)
    return pl.pallas_call(
        kernel,
        out_shape=(jax.ShapeDtypeStruct((ROWS, D), F32), jax.ShapeDtypeStruct((ROWS, D), F32)),
        in_specs=[anywhere, anywhere, inside, inside],
        out_specs=(inside, inside),
        scratch_shapes=scratch,
        compiler_params=pltpu.CompilerParams(collective_id=0, has_side_effects=True, vmem_limit_bytes=60 << 20),
        name="sinkhorn_back",
    )(embeddings, prototypes, row_cot.reshape(1, ROWS), col_cot.reshape(TILES, 128))


def solution(mesh):
    split = Mesh(mesh.devices.reshape(NX, NZ, NC, NY), ("x", "z", "c", "p"))
    rows = ("x", "z", "c")
    return jax.shard_map(
        step,
        mesh=split,
        in_specs=(P(rows, None), P("p", None), P(rows), P("p")),
        out_specs=(P(rows, None), P(("p",) + rows, None)),
        check_vma=False,
    )
```

time: 617 us -> 133 us (0.22); the launches traced: 605 us -> 133 us
  waiting for transfers between devices: 234 us -> 0 us
  blocking collectives: 212 us -> 0 us
  Pallas kernels: 0 us -> 129 us
  other arithmetic: 107 us -> 0 us
  matrix products: 27.7 us -> 0 us
  between operations: 14.5 us -> 0.64 us
    all_gather x12 -> x0, blocking collectives: 166 us -> none  [merged_by_axis(): pieces = jax.tree.map(lambda part: lax.all_gather(part, axis), x)]
    reduce_scatter x1 -> x0, waiting for transfers between devices: 157 us -> none  [shards(): lax.psum_scatter(product * score_scale, BATCH, scatter_dimension=0, tiled...]
    pallas_call x0 -> x1, Pallas kernels: none -> 129 us  [step(): pl.pallas_call(kernel, out_shape=(jax.ShapeDtypeStruct((ROWS, D), F32), j...]
    all_gather x1 -> x0, waiting for transfers between devices: 76.7 us -> none  [over_pieces(): parts = lax.all_gather(x, axis)]
    reduce_sum x11 -> x0, other arithmetic: 62.5 us -> none  [the longest x2 17.3 us: col_lse(): local_mass = jnp.sum(jnp.exp(shifted - local_peak[None, :]), axis=0)]
    all_to_all x5 -> x0, blocking collectives: 46 us -> none  [sent_to_all(): lax.all_to_all(jnp.broadcast_to(x[None], (length, *x.shape)), axis, 0, 0,...]
    dot_general x3 -> x0, matrix products: 27.7 us -> none  [the longest x1 11.5 us: shards(): lax.dot_general(embeddings, prototypes, (((1,), (1,)), ((), ())), preferr...]
    reduce_max x3 -> x0, other arithmetic: 22.5 us -> none  [the longest x2 15.3 us: col_lse(): local_peak = jnp.max(shifted, axis=0)]
  transfers between devices with their start and end apart: 2 -> 0, of which waited for: 2 -> 0; matrix products, arithmetic and copies ran while one was open for 1% -> 0% of each run, Pallas kernels for 0% -> 0%
where the time goes in v1:
time: 133 us
  Pallas kernels  129 us (97%)
  local copies, waits for them, and re-layouts  3.34 us (3%)
    pallas_call x1, Pallas kernels, step(): pl.pallas_call(kernel, out_shape=(jax.ShapeDtypeStruct((ROWS, D), F32), j...  129 us
    unnamed x2, local copies, waits for them, and re-layouts  3.34 us

profile of v1, /device:TPU:1, one launch (start us, length us, event | category | flops | bytes accessed | tf_op | source)
XLA Modules:
  0.0 132.6 jit_solution(659272850872974908)
XLA Ops:
  0.6 128.6 %sinkhorn_back.1 = (f32[256,256]{1,0:T(8,128)}, f32[256,256]{1,0:T(8,128)}) custom-call(bf16[256,256]{1,0:T(8,128)(2,1)} %emb_hbm.1, bf16[16384,256]{1,0:T(8,128)(2,1)} %protos_hbm.1, f32[1,256]{1,0:T(1,128)} %bitcast.3, f32[128,128]{1,0:T(8,128)} %bitcast.2), custom_call_target="tpu_custom_call" | custom-call | tf_op jit(solution)/shard_map/sinkhorn_back/pallas_call | solution.py:354
  129.2 1.7 %copy.8 = f32[256,256]{1,0:T(8,128)} copy(f32[256,256]{1,0:T(8,128)} %get-tuple-element.4) | data formatting | bytes 524288
  130.9 1.7 %copy.9 = f32[256,256]{1,0:T(8,128)} copy(f32[256,256]{1,0:T(8,128)} %get-tuple-element.5) | data formatting | bytes 524288

commit v2 on v1

--- a/solution.py
+++ b/solution.py
@@ -52,7 +52,7 @@
 
 
 def kernel(emb_hbm, protos_hbm, rcot_ref, ccot_ref, eg_ref, pg_ref,
-           S, PV, EA, MX, FB, UB, XB, CM, CS, W, A, H, LG, V, ADJ, RP, PG, PR, LB, AB, CB, DB, ADJ2,
+           S, PV, EA, MX, FB, UB, XB, CM, CS, W, A, H, LG, V, ADJ, RP, PG, PR, LB, AB, CB, DB, ADJ2, ST, T,
            rbuf, cloc, c1, c2, c3, G, Y, EB, EO,
            psem, esem, rs, rr, s1, r1, s2, r2, s3, r3, es_z, es_x, er, gs, gr, ys, yr, eb_s, eb_r, eo_s, eo_r, pr_s, pr_r):
     x, z, c, y = lax.axis_index("x"), lax.axis_index("z"), lax.axis_index("c"), lax.axis_index("p")
@@ -102,15 +102,28 @@
     MX[...] = jnp.full((ROWS, 128), -jnp.inf, F32)
     own.wait()
 
+    def fold(q, n):
+        for b in range(4):
+            at = slice(b * 64, (b + 1) * 64)
+            tiles = [T[n, at, j * 128:(j + 1) * 128] for j in range(4)]
+            old = MX[at, :]
+            new = jnp.maximum(jnp.maximum(jnp.maximum(tiles[0], tiles[1]), jnp.maximum(tiles[2], tiles[3])), old)
+            mass = XB[at, :] * jnp.exp2(old - new)
+            more = (jnp.exp2(tiles[0] - new) + jnp.exp2(tiles[1] - new)) + (jnp.exp2(tiles[2] - new) + jnp.exp2(tiles[3] - new))
+            XB[at, :] = mass + more
+            MX[at, :] = new
+            for j in range(4):
+                S[4 * q + j, at, :] = tiles[j]
+
+    def score(q, n):
+        at = pl.multiple_of(q * 512, 512)
+        T[n] = dot_nt(EA[x, z], PV[pl.ds(at, 512), :]) * SCALE2
+
     def score_chunk(q, _):
-        at = pl.multiple_of(q * 512, 512)
-        s = dot_nt(EA[x, z], PV[pl.ds(at, 512), :]) * SCALE2
-        m = MX[...]
-        for j in range(4):
-            t = s[:, j * 128:(j + 1) * 128]
-            S[4 * q + j] = t
-            m = jnp.maximum(m, t)
-        MX[...] = m
+        score(2 * q + 1, 1)
+        fold(2 * q, 0)
+        score(jnp.minimum(2 * q + 2, TILES // 4 - 1), 0)
+        fold(2 * q + 1, 1)
         return 0
 
     def x_stage(r):
@@ -123,24 +136,25 @@
     def z_stage(d):
         send(EA.at[x, z], EA.at[x, z], es_z.at[NZ - d], er.at[x, z], {"z": at_z(d)})
 
-    for q in range(8):
-        loads[q].wait()
-        lax.fori_loop(q * 4, q * 4 + 4, score_chunk, 0)
-        if q == 3:
-            pl.semaphore_wait(barrier, NY - 1 + NX * NC - 1 + NZ - 1)
-            for d in (1, 7, 2, 6):
-                z_stage(d)
-            x_stage(0)
-
-    def mass_tile(t, acc):
-        for j in range(2):
-            acc = acc + jnp.exp2(S[2 * t + j] - MX[...])
-        return acc
-
-    mass = lax.fori_loop(0, TILES // 2, mass_tile, jnp.zeros((ROWS, 128), F32))
+    XB[...] = jnp.zeros((ROWS, 128), F32)
+    loads[0].wait()
+    score(0, 0)
+
+    def part(q, _):
+        pltpu.make_async_copy(protos_hbm.at[pl.ds(q * step, step)], PV.at[pl.ds(q * step, step)], psem.at[q]).wait()
+        lax.fori_loop(q * 2 - 2, q * 2, score_chunk, 0)
+        return 0
+
+    lax.fori_loop(1, 4, part, 0)
+    pl.semaphore_wait(barrier, NY - 1 + NX * NC - 1 + NZ - 1)
+    for d in (1, 7, 2, 6):
+        z_stage(d)
+    x_stage(0)
+    lax.fori_loop(4, 8, part, 0)
+    lax.fori_loop(14, 16, score_chunk, 0)
     mt = MX[...].T
     top = jnp.max(mt, axis=0, keepdims=True)
-    loc = top + jnp.log(jnp.sum(mass.T * jnp.exp2(mt - top), axis=0, keepdims=True)) * LOG2E
+    loc = top + jnp.log(jnp.sum(XB[...].T * jnp.exp2(mt - top), axis=0, keepdims=True)) * LOG2E
 
     def row_all(i, row, combine):
         rbuf[i, y] = row
@@ -176,33 +190,65 @@
         return c3[i].reshape(TILES, 128)
 
     def row_pass():
-        def tile(t, acc):
-            for j in range(4):
-                acc = acc + S[4 * t + j] * W[pl.ds(4 * t + j, 1), :]
-            return acc
-        return row_form(lax.fori_loop(0, TILES // 4, tile, jnp.zeros((ROWS, 128), F32)))
+        for b in range(4):
+            at = slice(b * 64, (b + 1) * 64)
+
+            def tile(t, acc):
+                even, odd = acc
+                for j in range(0, 8, 2):
+                    even = even + S[8 * t + j, at, :] * W[pl.ds(8 * t + j, 1), :]
+                    odd = odd + S[8 * t + j + 1, at, :] * W[pl.ds(8 * t + j + 1, 1), :]
+                return even, odd
+
+            none = jnp.zeros((64, 128), F32)
+            even, odd = lax.fori_loop(0, TILES // 8, tile, (none, none))
+            MX[at, :] = even + odd
+        return row_form(MX[...])
 
     def col_pass(weights):
         def tile(t, _):
-            for j in range(2):
-                CS[pl.ds(2 * t + j, 1), :] = jnp.sum(S[2 * t + j] * weights[...], axis=0, keepdims=True)
+            acc = [None] * 4
+            for b in range(4):
+                at = slice(b * 64, (b + 1) * 64)
+                w = weights[at, :]
+                for j in range(4):
+                    term = S[4 * t + j, at, :] * w
+                    acc[j] = term if b == 0 else acc[j] + term
+            for j in range(4):
+                CS[pl.ds(4 * t + j, 1), :] = jnp.sum(acc[j], axis=0, keepdims=True)
             return 0
-        lax.fori_loop(0, TILES // 2, tile, 0)
+        lax.fori_loop(0, TILES // 4, tile, 0)
         return CS[...]
 
     f_one = -LOG2_B - row_all(0, loc, lse2)
     FB[...] = spread(f_one)
 
-    def plan_tile(t, _):
-        v = S[t] + FB[...]
-        m = jnp.max(v, axis=0, keepdims=True)
-        e = jnp.exp2(v - m)
-        S[t] = e
-        CM[pl.ds(t, 1), :] = m
-        CS[pl.ds(t, 1), :] = jnp.sum(e, axis=0, keepdims=True)
-        return 0
-
-    lax.fori_loop(0, TILES, plan_tile, 0)
+    def tops(t):
+        best = [None, None]
+        for b in range(4):
+            at = slice(b * 64, (b + 1) * 64)
+            f = FB[at, :]
+            for j in range(2):
+                here = S[t + j, at, :] + f
+                best[j] = here if b == 0 else jnp.maximum(best[j], here)
+        return tuple(jnp.max(m, axis=0, keepdims=True) for m in best)
+
+    def plan_tile(t, m):
+        later = tops(jnp.minimum(2 * t + 2, TILES - 2))
+        acc = [None, None]
+        for b in range(4):
+            at = slice(b * 64, (b + 1) * 64)
+            f = FB[at, :]
+            for j in range(2):
+                e = jnp.exp2(S[2 * t + j, at, :] + f - m[j])
+                S[2 * t + j, at, :] = e
+                acc[j] = e if b == 0 else acc[j] + e
+        for j in range(2):
+            CM[pl.ds(2 * t + j, 1), :] = m[j]
+            CS[pl.ds(2 * t + j, 1), :] = jnp.sum(acc[j], axis=0, keepdims=True)
+        return later
+
+    lax.fori_loop(0, TILES // 2, plan_tile, tops(0))
     big = col_all(0, CM[...] + jnp.log(CS[...]) * LOG2E, lse2, lambda: x_stage(1))
     LG[...] = big
     H[...] = jnp.exp2(CM[...] - big)
@@ -248,24 +294,39 @@
     CM[...] = jnp.exp2(CM[...]) * N_B
     RP[...] = jnp.zeros((ROWS, D), F32)
 
+    def adjoint_rows(q, n):
+        for b in range(8):
+            at = slice(b * 32, (b + 1) * 32)
+            ub, xb, yb = UB[at, :], XB[at, :], FB[at, :]
+            for j in range(8):
+                t = 8 * q + j
+                g = ub * A[pl.ds(t, 1), :] + xb * H[pl.ds(t, 1), :]
+                g = g + (yb * CM[pl.ds(t, 1), :] + W[pl.ds(t, 1), :])
+                ADJ[n, at, j * 128:(j + 1) * 128] = (S[t, at, :] * g).astype(BF16)
+
+    def row_grad(q, n):
+        at = pl.multiple_of(q * 1024, 1024)
+        RP[...] += jnp.dot(ADJ[n], PV[pl.ds(at, 1024), :], preferred_element_type=F32)
+
     def grad_chunk(q, _):
-        at = pl.multiple_of(q * 512, 512)
-        for j in range(4):
-            t = 4 * q + j
-            g = UB[...] * A[pl.ds(t, 1), :] + XB[...] * H[pl.ds(t, 1), :]
-            g = g + FB[...] * CM[pl.ds(t, 1), :] + W[pl.ds(t, 1), :]
-            ADJ[:, j * 128:(j + 1) * 128] = (S[t] * g).astype(BF16)
-        RP[...] += jnp.dot(ADJ[...], PV[pl.ds(at, 512), :], preferred_element_type=F32)
+        row_grad(2 * q - 1, 1)
+        adjoint_rows(2 * q, 0)
+        row_grad(2 * q, 0)
+        adjoint_rows(2 * q + 1, 1)
         return 0
 
-    half = COLS // 1024
-    lax.fori_loop(0, half, grad_chunk, 0)
+    adjoint_rows(0, 0)
+    row_grad(0, 0)
+    adjoint_rows(1, 1)
+    half = COLS // 4096
+    lax.fori_loop(1, half, grad_chunk, 0)
     for d in range(1, NZ):
         f = at_z(d)
         landed(Y.at[x, f], ys.at[0, d], gr.at[NX + x, f], {"z": f})
     for d in range(1, NX):
         send(Y.at[x], Y.at[x], ys.at[1, d], yr.at[1, x], {"x": at_x(d)})
     lax.fori_loop(half, 2 * half, grad_chunk, 0)
+    row_grad(4 * half - 1, 1)
     piece = ROWS // NY
 
     def quarter(j):
@@ -294,21 +355,47 @@
             zb = at_z(r)
             landed(EA.at[f, zb], es_x.at[r, d], er.at[f, zb], {"x": f})
 
-    def back_block(o, _):
+    def back_scores(o, n):
+        s = dot_nt(pown[...], EA[o // NZ, o % NZ]) * SCALE2
+        ST[n] = s
+
+    def back_adjoint(o, n, m):
         xb, zb = o // NZ, o % NZ
-        s = dot_nt(pown[...], EA[xb, zb]) * SCALE2
-        for j in range(4):
-            at = slice(j * 128, (j + 1) * 128)
-            for n in range(2):
-                e = jnp.exp2(s[at, n * 128:(n + 1) * 128] + G[xb, zb, n:n + 1] - LB[at, :])
-                g = AB[at, :] * G[xb, zb, 2 + n:3 + n] + G[xb, zb, 4 + n:5 + n]
-                g = g + CB[at, :] + DB[at, :] * Y[xb, zb, n:n + 1]
-                ADJ2[at, n * 128:(n + 1) * 128] = (e * g).astype(BF16)
-        PG[...] += jnp.dot(ADJ2[...], EA[xb, zb], preferred_element_type=F32)
+        for b in range(16):
+            at = slice(b * 32, (b + 1) * 32)
+            l, a, g0, d = LB[at, :], AB[at, :], CB[at, :], DB[at, :]
+            for i in range(2):
+                to = slice(i * 128, (i + 1) * 128)
+                e = jnp.exp2((ST[n, at, to] - l) + G[xb, zb, i:i + 1])
+                g = (a * G[xb, zb, 2 + i:3 + i] + G[xb, zb, 4 + i:5 + i]) + (g0 + d * Y[xb, zb, i:i + 1])
+                ADJ2[m, at, (n % 2) * 256 + i * 128:(n % 2) * 256 + (i + 1) * 128] = (e * g).astype(BF16)
+
+    def back_grad(o, m):
+        rows = EA[o // NZ, pl.ds(o % NZ, 2)].reshape(2 * ROWS, D)
+        PG[...] += jnp.dot(ADJ2[m], rows, preferred_element_type=F32)
+
+    def back_four(q, first):
+        o = 4 * q
+        if not first:
+            back_grad(o - 2, 1)
+        back_scores(o + 1, 1)
+        back_adjoint(o, 0, 0)
+        back_scores(o + 2, 2)
+        back_adjoint(o + 1, 1, 0)
+        back_grad(o, 0)
+        back_scores(o + 3, 3)
+        back_adjoint(o + 2, 2, 1)
+        back_scores(jnp.minimum(o + 4, NX * NZ - 1), 0)
+        back_adjoint(o + 3, 3, 1)
+
+    def back_block(q, _):
+        back_four(q, False)
         return 0
 
-    mid = NX * NZ // 2
-    lax.fori_loop(0, mid, back_block, 0)
+    mid = NX * NZ // 8
+    back_scores(0, 0)
+    back_four(0, True)
+    lax.fori_loop(1, mid, back_block, 0)
     for d in range(1, NY):
         f = at_y(d)
         landed(EB.at[f], eb_s.at[d], eb_r.at[f], {"p": f})
@@ -316,6 +403,7 @@
     for d in range(1, NY):
         send(EO.at[y], EO.at[y], eo_s.at[d], eo_r.at[y], {"p": at_y(d)})
     lax.fori_loop(mid, 2 * mid, back_block, 0)
+    back_grad(NX * NZ - 2, 1)
     there = PG.at[pl.ds(pl.multiple_of((1 - c) * ROWS, ROWS), ROWS)]
     send(there, PR, pr_s, pr_r, {"c": 1 - c})
     for d in range(1, NY):
@@ -337,8 +425,8 @@
         vm((TILES, ROWS, 128), F32), vm((COLS, D), BF16), vm((NX, NZ, ROWS, D), BF16),
         wide, wide, wide, wide,
         line, line, line, line, line, line, line,
-        vm((ROWS, 512), BF16), vm((ROWS, D), F32), vm((2 * ROWS, D), F32), vm((ROWS, D), F32),
-        vm((512, 128), F32), vm((512, 128), F32), vm((512, 128), F32), vm((512, 128), F32), vm((512, ROWS), BF16),
+        vm((2, ROWS, 1024), BF16), vm((ROWS, D), F32), vm((2 * ROWS, D), F32), vm((ROWS, D), F32),
+        vm((512, 128), F32), vm((512, 128), F32), vm((512, 128), F32), vm((512, 128), F32), vm((2, 512, 512), BF16), vm((4, 512, ROWS), F32), vm((2, ROWS, 512), F32),
         vm((4, NY, 1, ROWS), F32), vm((3, 8, TILES // 8, 128), F32), vm((3, 8, TILES // 8, 128), F32),
         vm((3, NZ, TILES // 8, 128), F32), vm((3, 8, TILES // 8, 128), F32),
         vm((NX, NZ, 8, 128), F32), vm((NX, NZ, 2, 128), F32),

time: 133 us -> 114 us (0.86)
  Pallas kernels: 129 us -> 110 us
    pallas_call x1, Pallas kernels: 129 us -> 110 us  [step(): pl.pallas_call(kernel, out_shape=(jax.ShapeDtypeStruct((ROWS, D), F32), j...]
where the time goes in v2:
time: 114 us
  Pallas kernels  110 us (96%)
  local copies, waits for them, and re-layouts  3.34 us (3%)
    pallas_call x1, Pallas kernels, step(): pl.pallas_call(kernel, out_shape=(jax.ShapeDtypeStruct((ROWS, D), F32), j...  110 us
    unnamed x2, local copies, waits for them, and re-layouts  3.34 us

profile of v2, /device:TPU:1, one launch (start us, length us, event | category | flops | bytes accessed | tf_op | source)
XLA Modules:
  0.0 113.9 jit_solution(2704941422743379569)
XLA Ops:
  0.6 109.9 %sinkhorn_back.1 = (f32[256,256]{1,0:T(8,128)}, f32[256,256]{1,0:T(8,128)}) custom-call(bf16[256,256]{1,0:T(8,128)(2,1)} %emb_hbm.1, bf16[16384,256]{1,0:T(8,128)(2,1)} %protos_hbm.1, f32[1,256]{1,0:T(1,128)} %bitcast.3, f32[128,128]{1,0:T(8,128)} %bitcast.2), custom_call_target="tpu_custom_call" | custom-call | tf_op jit(solution)/shard_map/sinkhorn_back/pallas_call | solution.py:442
  110.5 1.7 %copy.8 = f32[256,256]{1,0:T(8,128)} copy(f32[256,256]{1,0:T(8,128)} %get-tuple-element.4) | data formatting | bytes 524288
  112.2 1.7 %copy.9 = f32[256,256]{1,0:T(8,128)} copy(f32[256,256]{1,0:T(8,128)} %get-tuple-element.5) | data formatting | bytes 524288

commit v3 on v2

v3 whole, which is shorter than its diff:
```python
import math

import jax
import jax.numpy as jnp
from jax import lax
from jax.experimental import pallas as pl
from jax.experimental.pallas import tpu as pltpu
from jax.sharding import Mesh
from jax.sharding import PartitionSpec as P

MESH = pl.DeviceIdType.MESH
LOG2E = math.log2(math.e)
SCALE = 4.0
SCALE2 = SCALE * LOG2E
F32 = jnp.float32
BF16 = jnp.bfloat16
NX, NZ, NC, NY = 4, 8, 2, 4
ROWS, COLS, WIDTH = 256, 16384, 256
TILES = COLS // 128
GROUP = TILES // 8
FAR_FIRST = ((2, 0), (2, 1), (1, 0), (1, 1), (3, 0), (3, 1), (0, 1))
LOG2_B = math.log2(ROWS * NX * NZ * NC)
N_B = float(ROWS * NX * NZ * NC)
N_K = float(COLS * NY)


def dot_nt(a, b):
    return lax.dot_general(a, b, (((1,), (1,)), ((), ())), preferred_element_type=F32)


def lse2(parts):
    top = parts[0]
    for p in parts[1:]:
        top = jnp.maximum(top, p)
    mass = jnp.exp2(parts[0] - top)
    for p in parts[1:]:
        mass = mass + jnp.exp2(p - top)
    return top + jnp.log(mass) * LOG2E


def total(parts):
    out = parts[0]
    for p in parts[1:]:
        out = out + p
    return out


def row_form(acc):
    return jnp.sum(acc.T, axis=0, keepdims=True)


def spread(row):
    return jnp.broadcast_to(row, (128, row.shape[1])).T


def kernel(emb_hbm, protos_hbm, rcot_ref, ccot_ref, eg_ref, pg_ref,
           S, PV, EA, MX, FB, UB, XB, CM, CS, W, D, NB, LG, V, ADJ, RP, PG, PR, LB, AB, CB, DB, ADJ2, NP, T,
           rbuf, cloc, c1, c2, c3, G, Y, FG, EB, EO,
           psem, esem, rs, rr, s1, r1, s2, r2, s3, r3, es_z, es_x, es_y, er, gs, gr, ys, yr, fs, fr, eb_s, eb_r, eo_s, eo_r, pr_s, pr_r):
    x, z, c, y = lax.axis_index("x"), lax.axis_index("z"), lax.axis_index("c"), lax.axis_index("p")
    k = x * NC + c
    sent = []

    def send(src, dst, ssem, rsem, where):
        copy = pltpu.make_async_remote_copy(src_ref=src, dst_ref=dst, send_sem=ssem, recv_sem=rsem,
                                            device_id=where, device_id_type=MESH)
        copy.start()
        sent.append(copy)

    def landed(ref, ssem, rsem, where):
        pltpu.make_async_remote_copy(src_ref=ref, dst_ref=ref, send_sem=ssem, recv_sem=rsem,
                                     device_id=where, device_id_type=MESH).wait_recv()

    def at_y(d):
        return (y + d % NY) % NY

    def at_z(d):
        return (z + d) % NZ

    def at_x(d):
        return (x + d) % NX

    def at_k(d):
        return (k + d) % (NX * NC)

    def xc(kk):
        return {"x": kk // NC, "c": kk % NC}

    barrier = pltpu.get_barrier_semaphore()
    for d in range(1, NY):
        pl.semaphore_signal(barrier, inc=1, device_id={"p": at_y(d)}, device_id_type=MESH)
    for d in range(1, NX * NC):
        pl.semaphore_signal(barrier, inc=1, device_id=xc(at_k(d)), device_id_type=MESH)
    for d in range(1, NZ):
        pl.semaphore_signal(barrier, inc=1, device_id={"z": at_z(d)}, device_id_type=MESH)

    own = pltpu.make_async_copy(emb_hbm, EA.at[x, z], esem)
    own.start()
    step = COLS // 8
    loads = [pltpu.make_async_copy(protos_hbm.at[pl.ds(q * step, step)], PV.at[pl.ds(q * step, step)], psem.at[q])
             for q in range(8)]
    for q in loads:
        q.start()
    MX[...] = jnp.full((ROWS, 128), -jnp.inf, F32)
    own.wait()

    def fold(q, n):
        for b in range(4):
            at = slice(b * 64, (b + 1) * 64)
            tiles = [T[n, at, j * 128:(j + 1) * 128] for j in range(4)]
            old = MX[at, :]
            new = jnp.maximum(jnp.maximum(jnp.maximum(tiles[0], tiles[1]), jnp.maximum(tiles[2], tiles[3])), old)
            mass = XB[at, :] * jnp.exp2(old - new)
            more = (jnp.exp2(tiles[0] - new) + jnp.exp2(tiles[1] - new)) + (jnp.exp2(tiles[2] - new) + jnp.exp2(tiles[3] - new))
            XB[at, :] = mass + more
            MX[at, :] = new
            for j in range(4):
                S[4 * q + j, at, :] = tiles[j]

    def score(q, n):
        at = pl.multiple_of(q * 512, 512)
        T[n] = dot_nt(EA[x, z], PV[pl.ds(at, 512), :]) * SCALE2

    def score_chunk(q, _):
        score(2 * q + 1, 1)
        fold(2 * q, 0)
        score(jnp.minimum(2 * q + 2, TILES // 4 - 1), 0)
        fold(2 * q + 1, 1)
        return 0

    parity = y % 2

    def offset(n, p):
        return (p, 2 + 5 * p, 6 - 3 * p, 4 + p)[n]

    def z_copy(n, there):
        return pltpu.make_async_remote_copy(
            src_ref=EA.at[x, z], dst_ref=EA.at[x, z], send_sem=es_z.at[n], recv_sem=er.at[x, z],
            device_id={"z": there}, device_id_type=MESH)

    def z_stage(n):
        there = at_z(NZ - offset(n, parity))
        if n:
            z_copy(n, there).start()
        else:
            @pl.when(parity == 1)
            def _():
                z_copy(n, there).start()

    def z_landed(n):
        f = at_z(offset(n, parity))
        if n:
            landed(EA.at[x, f], es_z.at[n], er.at[x, f], {"z": f})
        else:
            @pl.when(parity == 1)
            def _():
                landed(EA.at[x, f], es_z.at[n], er.at[x, f], {"z": f})

    def z_sent(n):
        if n:
            z_copy(n, at_z(1)).wait_send()
        else:
            @pl.when(parity == 1)
            def _():
                z_copy(n, at_z(1)).wait_send()

    def x_stage(n):
        z_landed(n)
        zb = at_z(offset(n, parity))
        for d in range(1, NX):
            send(EA.at[x, zb], EA.at[x, zb], es_x.at[n, d], er.at[x, zb], {"x": at_x(d)})

    def y_first(zb):
        return pltpu.make_async_remote_copy(
            src_ref=EA.at[x, zb], dst_ref=EA.at[x, zb], send_sem=es_y.at[0, 0], recv_sem=er.at[x, zb],
            device_id={"p": at_y(1)}, device_id_type=MESH)

    def y_stage(n):
        zb = at_z(offset(n, parity))
        if n:
            send(EA.at[x, zb], EA.at[x, zb], es_y.at[n, 0], er.at[x, zb], {"p": at_y(1)})
        else:
            @pl.when(parity == 1)
            def _():
                y_first(zb).start()

        for d in range(1, NX):
            f = at_x(d)
            landed(EA.at[f, zb], es_x.at[n, d], er.at[f, zb], {"x": f})
            send(EA.at[f, zb], EA.at[f, zb], es_y.at[n, d], er.at[f, zb], {"p": at_y(1 if d < 2 else -1)})

    XB[...] = jnp.zeros((ROWS, 128), F32)
    loads[0].wait()
    score(0, 0)

    def part(q, _):
        pltpu.make_async_copy(protos_hbm.at[pl.ds(q * step, step)], PV.at[pl.ds(q * step, step)], psem.at[q]).wait()
        lax.fori_loop(q * 2 - 2, q * 2, score_chunk, 0)
        return 0

    lax.fori_loop(1, 4, part, 0)
    pl.semaphore_wait(barrier, NY - 1 + NX * NC - 1 + NZ - 1)
    for n in range(4):
        z_stage(n)
    lax.fori_loop(4, 8, part, 0)
    x_stage(0)
    lax.fori_loop(14, 16, score_chunk, 0)
    mt = MX[...].T
    top = jnp.max(mt, axis=0, keepdims=True)
    loc = top + jnp.log(jnp.sum(XB[...].T * jnp.exp2(mt - top), axis=0, keepdims=True)) * LOG2E

    def row_all(i, row, combine, fill):
        rbuf[i, y] = row
        for d in range(1, NY):
            send(rbuf.at[i, y], rbuf.at[i, y], rs.at[i, d], rr.at[i, y], {"p": at_y(d)})
        fill()
        for d in range(1, NY):
            f = at_y(d)
            landed(rbuf.at[i, f], rs.at[i, d], rr.at[i, f], {"p": f})
        return combine([rbuf[i, j] for j in range(NY)])

    def peers():
        for j, (dx, dc) in enumerate(FAR_FIRST):
            xx, cc = at_x(dx), (c + dc) % NC
            yield j, xx * NC + cc, {"x": xx, "c": cc}

    def col_round(i, piece, combine, fill_one, fill_two, use):
        for j, f, where in peers():
            cloc[i, f] = piece(f)
            send(cloc.at[i, f], c1.at[i, k], s1.at[i, j], r1.at[i, k], where)
        c1[i, k] = piece(k)
        fill_one()
        for j, f, where in peers():
            landed(c1.at[i, f], s1.at[i, j], r1.at[i, f], where)
        c2[i, z] = combine([c1[i, j] for j in range(8)])
        for d in range(1, NZ):
            send(c2.at[i, z], c2.at[i, z], s2.at[i, d], r2.at[i, z], {"z": at_z(d)})
        fill_two()
        for d in range(1, NZ):
            f = at_z(d)
            landed(c2.at[i, f], s2.at[i, d], r2.at[i, f], {"z": f})
        c3[i, k] = combine([c2[i, j] for j in range(NZ)])
        for j, f, where in peers():
            send(c3.at[i, k], c3.at[i, k], s3.at[i, j], r3.at[i, k], where)
        MX[...] = jnp.zeros((ROWS, 128), F32)
        use(k, c3[i, k])
        for j, f, where in list(peers())[::-1]:
            landed(c3.at[i, f], s3.at[i, j], r3.at[i, f], where)
            use(f, c3[i, f])
        return row_form(MX[...])

    def group(f):
        return pl.ds(pl.multiple_of(f * GROUP, GROUP), GROUP)

    def row_add(f, keep):
        def block(b, _):
            at = pl.ds(pl.multiple_of(b * 64, 64), 64)
            acc = [MX[at, :], jnp.zeros((64, 128), F32)]
            for j in range(GROUP):
                t = f * GROUP + j
                term = S[t, at, :] * W[pl.ds(t, 1), :]
                if keep:
                    S[t, at, :] = term
                acc[j % 2] = acc[j % 2] + term
            MX[at, :] = acc[0] + acc[1]
            return 0
        lax.fori_loop(0, 4, block, 0)

    def col_piece(weights, f):
        def tile(q, _):
            t = f * GROUP + 4 * q
            acc = [None] * 4
            for b in range(4):
                at = slice(b * 64, (b + 1) * 64)
                w = weights[at, :]
                for j in range(4):
                    term = S[t + j, at, :] * w
                    acc[j] = term if b == 0 else acc[j] + term
            for j in range(4):
                CS[pl.ds(t + j, 1), :] = jnp.sum(acc[j], axis=0, keepdims=True)
            return 0
        lax.fori_loop(0, GROUP // 4, tile, 0)
        return CS[group(f), :]

    def bulk_one():
        pass

    f_one = -LOG2_B - row_all(0, loc, lse2, bulk_one)
    FB[...] = spread(f_one)
    FG[x, z, 0:1] = f_one[:, :128]
    FG[x, z, 1:2] = f_one[:, 128:]
    for d in range(1, NZ):
        send(FG.at[x, z], FG.at[x, z], fs.at[0, d], fr.at[0, z], {"z": at_z(d)})

    def tops(t):
        best = [None, None]
        for b in range(4):
            at = slice(b * 64, (b + 1) * 64)
            f = FB[at, :]
            for j in range(2):
                here = S[t + j, at, :] + f
                best[j] = here if b == 0 else jnp.maximum(best[j], here)
        return tuple(jnp.max(m, axis=0, keepdims=True) for m in best)

    def plan_piece(f):
        start = f * GROUP

        def tile(q, m):
            t = start + 2 * q
            later = tops(jnp.minimum(t + 2, start + GROUP - 2))
            acc = [None, None]
            for b in range(4):
                at = slice(b * 64, (b + 1) * 64)
                fb = FB[at, :]
                for j in range(2):
                    e = jnp.exp2(S[t + j, at, :] + fb - m[j])
                    S[t + j, at, :] = e
                    acc[j] = e if b == 0 else acc[j] + e
            for j in range(2):
                CM[pl.ds(t + j, 1), :] = m[j]
                CS[pl.ds(t + j, 1), :] = jnp.sum(acc[j], axis=0, keepdims=True)
            return later

        lax.fori_loop(0, GROUP // 2, tile, tops(start))
        at = group(f)
        return CM[at, :] + jnp.log(CS[at, :]) * LOG2E

    chip = x * NZ + z
    pown = PV.at[pl.ds(pl.multiple_of(chip * 512, 512), 512)]

    def own_cols(ref, out):
        for j in range(4):
            out[j * 128:(j + 1) * 128, :] = spread(ref[pl.ds(chip * 4 + j, 1), :])

    def back_plan(n, theirs):
        zb = at_z(offset(n, 1 - parity if theirs else parity))
        if theirs:
            if n == 0:
                @pl.when(parity == 0)
                def _():
                    y_first(zb).wait_recv()

            for d in range(1 if n == 0 else 0, NX):
                f = at_x(d)
                landed(EA.at[f, zb], es_y.at[n, d], er.at[f, zb], {"p": at_y(-1 if d < 2 else 1)})

        def block(xb, _):
            s = dot_nt(pown[...], EA[xb, zb]) * SCALE2
            for i in range(2):
                NP[xb * NZ + zb, :, i * 128:(i + 1) * 128] = jnp.exp2(
                    (s[:, i * 128:(i + 1) * 128] - LB[...]) + FG[xb, zb, i:i + 1])
            return 0

        lax.fori_loop(0, NX, block, 0)

    def share_f():
        y_stage(0)
        for d in range(1, NZ):
            f = at_z(d)
            landed(FG.at[x, f], fs.at[0, d], fr.at[0, f], {"z": f})
        for d in range(1, NX):
            send(FG.at[x], FG.at[x], fs.at[1, d], fr.at[1, x], {"x": at_x(d)})

    def use_one(f, big):
        at = group(f)
        LG[at, :] = big
        D[at, :] = jnp.exp2(big) * N_B
        W[at, :] = jnp.exp2(CM[at, :] - big)
        row_add(f, True)

    def fill_row_two():
        x_stage(2)
        own_cols(LG, LB)
        for d in range(1, NX):
            f = at_x(d)
            landed(FG.at[f], fs.at[1, d], fr.at[1, f], {"x": f})
        back_plan(0, False)

    mass = col_round(0, plan_piece, lse2, share_f, lambda: x_stage(1), use_one)
    u = (N_K / N_B) / row_all(1, mass, total, fill_row_two)
    UB[...] = spread(u)

    def use_two(f, col):
        at = group(f)
        V[at, :] = ccot_ref[at, :] * (-1.0 / col)
        W[at, :] = V[at, :]
        row_add(f, False)

    def fill_col_two():
        x_stage(3)
        y_stage(2)
        back_plan(0, True)

    def fill_row_three():
        own_cols(V, AB)
        back_plan(2, False)

    def fill_col_two_first():
        y_stage(1)
        back_plan(1, False)

    moved = col_round(1, lambda f: col_piece(UB, f), total, fill_col_two_first, fill_col_two, use_two)
    bar_two = rcot_ref[...] + u * row_all(2, moved, total, fill_row_three)
    xr = bar_two * u
    XB[...] = spread(xr)
    xn = xr * -(N_B / N_K)
    for j, vec in enumerate((u, xn)):
        G[x, z, 2 * j:2 * j + 1] = vec[:, :128]
        G[x, z, 2 * j + 1:2 * j + 2] = vec[:, 128:]
    for d in range(1, NZ):
        send(G.at[x, z], G.at[x, z], gs.at[0, d], gr.at[x, z], {"z": at_z(d)})

    def use_three(f, col):
        at = group(f)
        NB[at, :] = col * (N_B / N_K)
        W[at, :] = NB[at, :]
        row_add(f, False)

    def fill_col_three():
        for d in range(1, NZ):
            f = at_z(d)
            landed(G.at[x, f], gs.at[0, d], gr.at[x, f], {"z": f})
        for d in range(1, NX):
            send(G.at[x], G.at[x], gs.at[1, d], yr.at[0, x], {"x": at_x(d)})
        back_plan(3, False)
        back_plan(2, True)

    def fill_row_four():
        XB[...] = XB[...] * -(N_B / N_K)
        own_cols(NB, CB)
        own_cols(D, DB)
        back_plan(3, True)

    def fill_col_three_first():
        y_stage(3)
        back_plan(1, True)

    last = col_round(2, lambda f: col_piece(XB, f), total, fill_col_three_first, fill_col_three, use_three)
    yn = -row_all(3, last, total, fill_row_four)
    Y[x, z, 0:1] = yn[:, :128]
    Y[x, z, 1:2] = yn[:, 128:]
    for d in range(1, NZ):
        send(Y.at[x, z], Y.at[x, z], ys.at[0, d], gr.at[NX + x, z], {"z": at_z(d)})
    FB[...] = spread(yn)
    RP[...] = jnp.zeros((ROWS, WIDTH), F32)

    HALF = ROWS // 2
    piece = ROWS // NY

    def adjoint_rows(q, n, h):
        for b in range(4):
            at = slice(h * HALF + b * 32, h * HALF + (b + 1) * 32)
            ub, xb, yb = UB[at, :], XB[at, :], FB[at, :]
            for j in range(8):
                t = 8 * q + j
                g = (ub * V[pl.ds(t, 1), :] + xb) + (yb * D[pl.ds(t, 1), :] + NB[pl.ds(t, 1), :])
                ADJ[n, b * 32:(b + 1) * 32, j * 128:(j + 1) * 128] = (S[t, at, :] * g).astype(BF16)

    def row_grad(q, n, h):
        at = pl.multiple_of(q * 1024, 1024)
        rows = slice(h * HALF, (h + 1) * HALF)
        RP[rows, :] += jnp.dot(ADJ[n], PV[pl.ds(at, 1024), :], preferred_element_type=F32)

    def grad_half(h):
        def grad_chunk(q, _):
            row_grad(2 * q - 1, 1, h)
            adjoint_rows(2 * q, 0, h)
            row_grad(2 * q, 0, h)
            adjoint_rows(2 * q + 1, 1, h)
            return 0

        adjoint_rows(0, 0, h)
        row_grad(0, 0, h)
        adjoint_rows(1, 1, h)
        lax.fori_loop(1, COLS // 2048, grad_chunk, 0)
        row_grad(COLS // 1024 - 1, 1, h)
        for j in range(2 * h, 2 * h + 2):
            EB[j, y] = RP[j * piece:(j + 1) * piece, :]

            @pl.when(y != j)
            def _():
                eb_copy(j).start()

    def eb_copy(j):
        return pltpu.make_async_remote_copy(
            src_ref=EB.at[j, y], dst_ref=EB.at[j, y], send_sem=eb_s.at[j], recv_sem=eb_r.at[y],
            device_id={"p": j}, device_id_type=MESH)

    grad_half(0)
    for d in range(1, NZ):
        f = at_z(d)
        landed(Y.at[x, f], ys.at[0, d], gr.at[NX + x, f], {"z": f})
    for d in range(1, NX):
        send(Y.at[x], Y.at[x], ys.at[1, d], yr.at[1, x], {"x": at_x(d)})
    grad_half(1)

    PG[...] = jnp.zeros((2 * ROWS, WIDTH), F32)
    for d in range(1, NX):
        f = at_x(d)
        landed(G.at[f], gs.at[1, d], yr.at[0, f], {"x": f})
        landed(Y.at[f], ys.at[1, d], yr.at[1, f], {"x": f})

    def back_adjoint(o, n, m):
        xb, zb = o // NZ, o % NZ
        for b in range(16):
            at = slice(b * 32, (b + 1) * 32)
            a, g0, d = AB[at, :], CB[at, :], DB[at, :]
            for i in range(2):
                g = (a * G[xb, zb, i:i + 1] + G[xb, zb, 2 + i:3 + i]) + (g0 + d * Y[xb, zb, i:i + 1])
                to = slice(n * 256 + i * 128, n * 256 + (i + 1) * 128)
                ADJ2[m, at, to] = (NP[o, at, i * 128:(i + 1) * 128] * g).astype(BF16)

    def back_grad(o, m):
        rows = EA[o // NZ, pl.ds(o % NZ, 2)].reshape(2 * ROWS, WIDTH)
        PG[...] += jnp.dot(ADJ2[m], rows, preferred_element_type=F32)

    def back_block(q, _):
        o = 4 * q
        back_grad(o - 2, 1)
        back_adjoint(o, 0, 0)
        back_adjoint(o + 1, 1, 0)
        back_grad(o, 0)
        back_adjoint(o + 2, 0, 1)
        back_adjoint(o + 3, 1, 1)
        return 0

    def share_rows():
        for d in range(1, NY):
            f = at_y(d)
            landed(EB.at[y, f], eb_s.at[0], eb_r.at[f], {"p": f})
        EO[y] = total([EB[y, j] for j in range(NY)]) * SCALE
        for d in range(1, NY):
            send(EO.at[y], EO.at[y], eo_s.at[d], eo_r.at[y], {"p": at_y(d)})

    back_adjoint(0, 0, 0)
    back_adjoint(1, 1, 0)
    back_grad(0, 0)
    back_adjoint(2, 0, 1)
    back_adjoint(3, 1, 1)
    lax.fori_loop(1, 4, back_block, 0)
    share_rows()
    lax.fori_loop(4, NX * NZ // 4, back_block, 0)
    back_grad(NX * NZ - 2, 1)
    there = PG.at[pl.ds(pl.multiple_of((1 - c) * ROWS, ROWS), ROWS)]
    send(there, PR, pr_s, pr_r, {"c": 1 - c})
    for d in range(1, NY):
        f = at_y(d)
        landed(EO.at[f], eo_s.at[d], eo_r.at[f], {"p": f})
    eg_ref[...] = EO[...].reshape(ROWS, WIDTH)
    landed(PR, pr_s, pr_r, {"c": 1 - c})
    pg_ref[...] = (PG[pl.ds(pl.multiple_of(c * ROWS, ROWS), ROWS), :] + PR[...]) * SCALE
    @pl.when(parity == 1)
    def _():
        y_first(z).wait_send()

    for n in range(4):
        z_sent(n)

        @pl.when(y != n)
        def _():
            eb_copy(n).wait_send()
    for copy in sent:
        copy.wait_send()


def step(embeddings, prototypes, row_cot, col_cot):
    vm = pltpu.VMEM
    dma = pltpu.SemaphoreType.DMA
    wide = vm((ROWS, 128), F32)
    line = vm((TILES, 128), F32)
    scratch = [
        vm((TILES, ROWS, 128), F32), vm((COLS, WIDTH), BF16), vm((NX, NZ, ROWS, WIDTH), BF16),
        wide, wide, wide, wide,
        line, line, line, line, line, line, line,
        vm((2, ROWS // 2, 1024), BF16), vm((ROWS, WIDTH), F32), vm((2 * ROWS, WIDTH), F32), vm((ROWS, WIDTH), F32),
        vm((512, 128), F32), vm((512, 128), F32), vm((512, 128), F32), vm((512, 128), F32), vm((2, 512, 512), BF16), vm((NX * NZ, 512, ROWS), F32), vm((2, ROWS, 512), F32),
        vm((4, NY, 1, ROWS), F32), vm((3, 8, TILES // 8, 128), F32), vm((3, 8, TILES // 8, 128), F32),
        vm((3, NZ, TILES // 8, 128), F32), vm((3, 8, TILES // 8, 128), F32),
        vm((NX, NZ, 4, 128), F32), vm((NX, NZ, 2, 128), F32), vm((NX, NZ, 2, 128), F32),
        vm((NY, NY, ROWS // NY, WIDTH), F32), vm((NY, ROWS // NY, WIDTH), F32),
        dma((8,)), dma(()), dma((4, NY)), dma((4, NY)),
        dma((3, 8)), dma((3, 8)), dma((3, 8)), dma((3, 8)), dma((3, 8)), dma((3, 8)),
        dma((4,)), dma((4, NX)), dma((4, NX)), dma((NX, NZ)), dma((2, NZ)), dma((2 * NX, NZ)),
        dma((2, NZ)), dma((2, NX)), dma((2, NZ)), dma((2, NZ)),
        dma((NY,)), dma((NY,)), dma((NY,)), dma((NY,)), dma(()), dma(()),
    ]
    anywhere = pl.BlockSpec(memory_space=pl.ANY)
    inside = pl.BlockSpec(memory_space=pltpu.VMEM)
    return pl.pallas_call(
        kernel,
        out_shape=(jax.ShapeDtypeStruct((ROWS, WIDTH), F32), jax.ShapeDtypeStruct((ROWS, WIDTH), F32)),
        in_specs=[anywhere, anywhere, inside, inside],
        out_specs=(inside, inside),
        scratch_shapes=scratch,
        compiler_params=pltpu.CompilerParams(collective_id=0, has_side_effects=True, vmem_limit_bytes=60 << 20),
        name="sinkhorn_back",
    )(embeddings, prototypes, row_cot.reshape(1, ROWS), col_cot.reshape(TILES, 128))


def solution(mesh):
    split = Mesh(mesh.devices.reshape(NX, NZ, NC, NY), ("x", "z", "c", "p"))
    rows = ("x", "z", "c")
    return jax.shard_map(
        step,
        mesh=split,
        in_specs=(P(rows, None), P("p", None), P(rows), P("p")),
        out_specs=(P(rows, None), P(("p",) + rows, None)),
        check_vma=False,
    )
```

time: 114 us -> 109 us (0.956)
  Pallas kernels: 110 us -> 105 us
    pallas_call x1, Pallas kernels: 110 us -> 105 us  [step(): pl.pallas_call(kernel, out_shape=(jax.ShapeDtypeStruct((ROWS, WIDTH), F32...]
where the time goes in v3:
time: 109 us; the launch traced here: 108 us
  Pallas kernels  105 us (96%)
  local copies, waits for them, and re-layouts  3.34 us (3%)
    pallas_call x1, Pallas kernels, step(): pl.pallas_call(kernel, out_shape=(jax.ShapeDtypeStruct((ROWS, WIDTH), F32...  105 us
    unnamed x2, local copies, waits for them, and re-layouts  3.34 us

profile of v3, /device:TPU:1, one launch (start us, length us, event | category | flops | bytes accessed | tf_op | source)
XLA Modules:
  0.0 108.5 jit_solution(1679664522913867880)
XLA Ops:
  0.6 104.5 %sinkhorn_back.1 = (f32[256,256]{1,0:T(8,128)}, f32[256,256]{1,0:T(8,128)}) custom-call(bf16[256,256]{1,0:T(8,128)(2,1)} %emb_hbm.1, bf16[16384,256]{1,0:T(8,128)(2,1)} %protos_hbm.1, f32[1,256]{1,0:T(1,128)} %bitcast.3, f32[128,128]{1,0:T(8,128)} %bitcast.2), custom_call_target="tpu_custom_call" | custom-call | tf_op jit(solution)/shard_map/sinkhorn_back/pallas_call | solution.py:589
  105.1 1.7 %copy.8 = f32[256,256]{1,0:T(8,128)} copy(f32[256,256]{1,0:T(8,128)} %get-tuple-element.4) | data formatting | bytes 524288
  106.8 1.7 %copy.9 = f32[256,256]{1,0:T(8,128)} copy(f32[256,256]{1,0:T(8,128)} %get-tuple-element.5) | data formatting | bytes 524288

commit v4 on v3

--- a/solution.py
+++ b/solution.py
@@ -354,6 +354,7 @@
         lax.fori_loop(0, NX, block, 0)
 
     def share_f():
+        x_stage(1)
         y_stage(0)
         for d in range(1, NZ):
             f = at_z(d)
@@ -376,7 +377,7 @@
             landed(FG.at[f], fs.at[1, d], fr.at[1, f], {"x": f})
         back_plan(0, False)
 
-    mass = col_round(0, plan_piece, lse2, share_f, lambda: x_stage(1), use_one)
+    mass = col_round(0, plan_piece, lse2, share_f, lambda: None, use_one)
     u = (N_K / N_B) / row_all(1, mass, total, fill_row_two)
     UB[...] = spread(u)
 
@@ -387,7 +388,6 @@
         row_add(f, False)
 
     def fill_col_two():
-        x_stage(3)
         y_stage(2)
         back_plan(0, True)
 
@@ -396,6 +396,7 @@
         back_plan(2, False)
 
     def fill_col_two_first():
+        x_stage(3)
         y_stage(1)
         back_plan(1, False)
 

time: 109 us -> 109 us (level)
  no operation moved by 1% of the time
where the time goes in v4:
time: 109 us; the launch traced here: 108 us
  Pallas kernels  104 us (95%)
  local copies, waits for them, and re-layouts  3.34 us (3%)
    pallas_call x1, Pallas kernels, step(): pl.pallas_call(kernel, out_shape=(jax.ShapeDtypeStruct((ROWS, WIDTH), F32...  104 us
    unnamed x2, local copies, waits for them, and re-layouts  3.34 us

profile of v4, /device:TPU:1, one launch (start us, length us, event | category | flops | bytes accessed | tf_op | source)
XLA Modules:
  0.0 108.4 jit_solution(14779281014255229608)
XLA Ops:
  0.6 104.4 %sinkhorn_back.1 = (f32[256,256]{1,0:T(8,128)}, f32[256,256]{1,0:T(8,128)}) custom-call(bf16[256,256]{1,0:T(8,128)(2,1)} %emb_hbm.1, bf16[16384,256]{1,0:T(8,128)(2,1)} %protos_hbm.1, f32[1,256]{1,0:T(1,128)} %bitcast.3, f32[128,128]{1,0:T(8,128)} %bitcast.2), custom_call_target="tpu_custom_call" | custom-call | tf_op jit(solution)/shard_map/sinkhorn_back/pallas_call | solution.py:590
  105.0 1.7 %copy.8 = f32[256,256]{1,0:T(8,128)} copy(f32[256,256]{1,0:T(8,128)} %get-tuple-element.4) | data formatting | bytes 524288
  106.7 1.7 %copy.9 = f32[256,256]{1,0:T(8,128)} copy(f32[256,256]{1,0:T(8,128)} %get-tuple-element.5) | data formatting | bytes 524288
